TPU v7x, 256 devices: a whole 4x4x8 slice. The times are simulated.
256 devices in a mesh: px: 4 (over z_lo), py: 8 (over y, core), ch: 8 (over z_hi, x).
Axes of the slice: x: 4, y: 4, z: 8 (z_hi: 2, z_lo: 4; z = z_hi * 4 + z_lo), core: 2. Of those that a mesh axis runs over, the one named last changes fastest.
Arguments:
- features: bfloat16 [128, 12, 8, 4, 512], P('ch', None, 'py', 'px'), may hold values from -6 to 6
- cotangent: bfloat16 [128, 12, 8, 4, 512], P('ch', None, 'py', 'px'), may hold values from -6 to 6
- weight: bfloat16 [3, 3, 128, 128], replicated, may hold values from -0.1875 to 0.1875
- edge_table: int32 [12, 4, 3], replicated, may hold values from 0 to 11, as said below
- corner_table: int32 [12, 4, 2], replicated, may hold values from 0 to 11, as said below
Outputs:
- activation: bfloat16 [128, 12, 8, 4, 512], P('ch', None, 'py', 'px')
- input_grad: bfloat16 [128, 12, 8, 4, 512], P('ch', None, 'py', 'px')
Inputs may be any that keep to these rules, and one draw needn't show every extreme that they name: edge_table[f, e] = (g, s, r): beyond edge e of face f lie the pixels of side s of face g, in reverse order if r = 1; every side of every face is named exactly once, and if (f, e) names (g, s) then (g, s) names (f, e) with the same r. corner_table[f, c] = (h, q): corner c of face f takes corner pixel q of face h; in each corner column every face appears once, and each q appears 12 times.
All inputs are finite; a program needn't handle non-finite values.
Results may differ from a plain program's by a relative error of at most 0.0049.
Values may be sent and summed in bfloat16 or wider, within the bound.
A program may use at most 192 MiB of HBM per device.

v0:
```python
import jax
import jax.numpy as jnp
from jax import lax
from jax.sharding import PartitionSpec as P

RB = 32


def with_halo(array, sides, width):
    for axis, dim in sides:
        size, length = (lax.axis_size(axis), array.shape[dim])
        up = [(i, (i + 1) % size) for i in range(size - 1)]
        down = [(j, i) for i, j in up]
        last = lax.slice_in_dim(array, length - width, length, axis=dim)
        leading = lax.slice_in_dim(array, 0, width, axis=dim)
        before = lax.ppermute(last, axis, up)
        after = lax.ppermute(leading, axis, down)
        array = jnp.concatenate([before, array, after], axis=dim)
    return array


def edge_strips(lines, edge_table, corner_table):
    chan_count = lines.shape[0]
    face_count = lines.shape[1]
    side_len = lines.shape[3]
    flat_lines = lines.reshape(chan_count, face_count * 4, side_len)
    pixels = jnp.stack(
        [lines[:, :, 0, 0], lines[:, :, 0, -1], lines[:, :, 1, 0], lines[:, :, 1, -1]], axis=2
    ).reshape(chan_count, face_count * 4)
    corner_index = corner_table[:, :, 0] * 4 + corner_table[:, :, 1]
    corner_vals = jnp.take(pixels, corner_index, axis=1)
    strips = []
    for edge_num, start_corner, end_corner in ((0, 0, 1), (1, 2, 3), (2, 0, 2), (3, 1, 3)):
        source_row = edge_table[:, edge_num, 0] * 4 + edge_table[:, edge_num, 1]
        strip_line = jnp.take(flat_lines, source_row, axis=1)
        flipped = (edge_table[:, edge_num, 2] == 1)[None, :, None]
        strip_line = jnp.where(flipped, strip_line[:, :, ::-1], strip_line)
        strips.append(
            jnp.concatenate(
                [
                    corner_vals[:, :, start_corner : start_corner + 1],
                    strip_line,
                    corner_vals[:, :, end_corner : end_corner + 1],
                ],
                axis=2,
            )
        )
    return strips


def face_lines_of(field, row_pos, col_pos, px_count, py_count):
    chan_block = field.shape[0]
    face_count = field.shape[1]
    col_len = field.shape[2]
    row_len = field.shape[3]
    side_len = row_len * px_count
    blank = jnp.zeros((chan_block, face_count, side_len), jnp.float32)

    def placed(values, offset, active):
        return jnp.where(
            active,
            lax.dynamic_update_slice_in_dim(blank, values.astype(jnp.float32), offset, 2),
            0.0,
        )

    contrib = jnp.stack(
        [
            placed(field[:, :, 0, :], row_pos * row_len, col_pos == 0),
            placed(field[:, :, -1, :], row_pos * row_len, col_pos == py_count - 1),
            placed(field[:, :, :, 0], col_pos * col_len, row_pos == 0),
            placed(field[:, :, :, -1], col_pos * col_len, row_pos == px_count - 1),
        ],
        axis=2,
    )
    return lax.psum(contrib.astype(jnp.bfloat16), ("px", "py"))


def pad_field(field, edge_table, corner_table):
    col_len = field.shape[2]
    row_len = field.shape[3]
    row_pos = lax.axis_index("px")
    col_pos = lax.axis_index("py")
    px_count = lax.axis_size("px")
    py_count = lax.axis_size("py")
    padded = with_halo(field, (("px", 3), ("py", 2)), 1)
    lines = face_lines_of(field, row_pos, col_pos, px_count, py_count)
    strips = edge_strips(lines, edge_table, corner_table)
    top_row = lax.dynamic_slice_in_dim(strips[0], row_pos * row_len, row_len + 2, 2)
    bottom_row = lax.dynamic_slice_in_dim(strips[1], row_pos * row_len, row_len + 2, 2)
    left_col = lax.dynamic_slice_in_dim(strips[2], col_pos * col_len, col_len + 2, 2)
    right_col = lax.dynamic_slice_in_dim(strips[3], col_pos * col_len, col_len + 2, 2)
    padded = padded.at[:, :, 0, :].set(jnp.where(col_pos == 0, top_row, padded[:, :, 0, :]))
    padded = padded.at[:, :, -1, :].set(
        jnp.where(col_pos == py_count - 1, bottom_row, padded[:, :, -1, :])
    )
    padded = padded.at[:, :, :, 0].set(jnp.where(row_pos == 0, left_col, padded[:, :, :, 0]))
    padded = padded.at[:, :, :, -1].set(
        jnp.where(row_pos == px_count - 1, right_col, padded[:, :, :, -1])
    )
    return padded


def forward_taps(padded, taps, out_cols, out_rows):
    summed = None
    for tap_row in range(3):
        for tap_col in range(3):
            window = padded[:, :, tap_row : tap_row + out_cols, tap_col : tap_col + out_rows]
            term_val = jnp.einsum(
                "oc,cfab->ofab", taps[tap_row, tap_col], window, preferred_element_type=jnp.float32
            )
            summed = term_val if summed is None else summed + term_val
    return summed


def backward_taps(padded, taps, out_cols, out_rows):
    summed = None
    for tap_row in range(3):
        for tap_col in range(3):
            window = padded[
                :, :, 2 - tap_row : 2 - tap_row + out_cols, 2 - tap_col : 2 - tap_col + out_rows
            ]
            term_val = jnp.einsum(
                "oc,ofab->cfab", taps[tap_row, tap_col], window, preferred_element_type=jnp.float32
            )
            summed = term_val if summed is None else summed + term_val
    return summed


def gate_outputs(preact, cotangent):
    sigmoid_val = jax.nn.sigmoid(preact)
    activation = (preact * sigmoid_val).astype(jnp.bfloat16)
    gated = (
        cotangent.astype(jnp.float32) * sigmoid_val * (1.0 + preact * (1.0 - sigmoid_val))
    ).astype(jnp.bfloat16)
    return (activation, gated)


def local(features, cotangent, weight, edge_table, corner_table):
    chan_block = features.shape[0]
    face_count = features.shape[1]
    tile_len = features.shape[4]
    row_len = RB
    col_len = tile_len // row_len
    features = features.reshape(chan_block, face_count, col_len, row_len)
    cotangent = cotangent.reshape(chan_block, face_count, col_len, row_len)
    ch_pos = lax.axis_index("ch")
    feat_pad = pad_field(features, edge_table, corner_table)
    own_taps = lax.dynamic_slice_in_dim(weight, ch_pos * chan_block, chan_block, 2)
    piece_taps = own_taps
    preact = forward_taps(
        lax.all_gather(feat_pad, "ch", axis=0, tiled=True), piece_taps, col_len, row_len
    )
    activation, gated = gate_outputs(preact, cotangent)
    grad_pad = pad_field(gated, edge_table, corner_table)
    input_taps = lax.dynamic_slice_in_dim(weight, ch_pos * chan_block, chan_block, 3)
    piece_taps = input_taps
    input_grad = backward_taps(
        lax.all_gather(grad_pad, "ch", axis=0, tiled=True), piece_taps, col_len, row_len
    ).astype(jnp.bfloat16)
    out_shape = (chan_block, face_count, 1, 1, tile_len)
    return (activation.reshape(out_shape), input_grad.reshape(out_shape))


def solution(mesh):
    return jax.shard_map(
        local,
        mesh=mesh,
        in_specs=(P("ch", None, "py", "px", None), P("ch", None, "py", "px", None), P(), P(), P()),
        out_specs=(P("ch", None, "py", "px", None), P("ch", None, "py", "px", None)),
        check_vma=False,
    )
```

profile of v0, /device:TPU:8, one launch (start us, length us, event | category | flops | bytes accessed | tf_op | source)
XLA Modules:
  0.0 1055.1 jit_solution(10775510683861696942)
XLA Ops:
  7.2 1.4 reshape.426
  9.9 1.4 convert_select_fusion.2
  11.2 3.0 copy.696
  14.2 1.8 copy.697
  16.1 2.7 select_n.196
  18.7 2.7 select_n.200
  23.1 2.6 copy.698
  27.0 7.1 collective-permute-start
  34.1 1.2 copy.686
  35.3 1.3 collective-permute-start.1
  39.3 1.6 copy.687
  41.3 1.6 copy.689
  43.6 1.9 collective-permute-start.2
  45.5 3.9 collective-permute-start.3
  49.5 1.4 collective-permute-done.3
  51.5 1.6 pad_maximum_fusion
  53.1 254.8 %all-reduce.3.cloned.1.call-done = bf16[16,12,4,128]{1,0,3,2:T(8,128)(2,1)} async-done(((bf16[16,12,4,128]{1,0,3,2:T(8,128)(2,1)}), bf16[16,12,4,128]{1,0,3,2:T(8,128)(2,1)}) %all-reduce.3.cloned.1.call-update) | async-done | bytes 196624 | tf_op jit(solution)/shard_map/psum | solution.py:75
  307.9 3.0 copy.702
  316.1 1.3 copy.704
  317.6 1.3 copy.705
  318.9 3.8 scatter.30
  323.1 1.3 copy.706
  325.5 1.3 copy.707
  326.8 18.3 %scatter.31 = bf16[16,12,18,34]{3,0,2,1:T(8,128)(2,1)S(1)} dynamic-update-slice(bf16[16,12,18,34]{3,0,2,1:T(8,128)(2,1)S(1)} %scatter.30, bf16[16,12,18,1]{3,0,2,1:T(8,128)(2,1)S(1)} %copy.707, s32[]{:T(128)} %constant.235.clone.1, s32[]{:T(128)} %constant.235.clone.1, s32[]{:T(128)} %constant.235.clone.1, s32[]{:T(128)} %constant.249.clone.1) | dynamic-update-slice | bytes 13828 | tf_op jit(solution)/shard_map/scatter | solution.py:97
  346.6 1.3 reshape.441
  347.9 162.8 %all-gather.3.cloned.1.call-done = bf16[128,12,18,34]{3,0,2,1:T(8,128)(2,1)} async-done(((bf16[16,12,18,34]{3,0,2,1:T(8,128)(2,1)}), bf16[128,12,18,34]{3,0,2,1:T(8,128)(2,1)}) %all-gather.3.cloned.1.call-update) | async-done | bytes 1880080 | tf_op jit(solution)/shard_map/all_gather | solution.py:151
  510.7 4.7 fusion.20
  515.5 1.8 fusion.24
  518.3 1.8 fusion.26
  521.0 1.8 fusion.30
  522.8 1.8 fusion.32
  524.6 2.0 fusion.18
  526.6 2.6 fusion.37
  529.2 1.7 convert_select_fusion.1
  531.6 2.3 copy.725
  535.1 1.2 copy.720
  536.3 2.2 collective-permute-start.4
  539.8 1.3 collective-permute-start.5
  541.1 1.9 select_n.220
  543.0 1.9 select_n.223
  545.7 2.6 copy.727
  548.4 1.3 copy.722
  549.7 1.3 copy.723
  551.1 1.9 collective-permute-start.6
  553.0 3.9 collective-permute-start.7
  556.9 1.5 collective-permute-done.7
  559.2 266.2 %all-reduce.5.cloned.1.call-done = bf16[16,12,4,128]{1,0,3,2:T(8,128)(2,1)} async-done(((bf16[16,12,4,128]{1,0,3,2:T(8,128)(2,1)}), bf16[16,12,4,128]{1,0,3,2:T(8,128)(2,1)}) %all-reduce.5.cloned.1.call-update) | async-done | bytes 196624 | tf_op jit(solution)/shard_map/psum | solution.py:75
  825.4 3.0 copy.731
  834.4 1.3 copy.732
  835.8 1.3 copy.733
  837.1 3.8 scatter.36
  841.2 1.3 copy.734
  842.9 1.3 copy.735
  844.2 18.6 %scatter.39 = bf16[16,12,18,34]{3,0,2,1:T(8,128)(2,1)S(1)} dynamic-update-slice(bf16[16,12,18,34]{3,0,2,1:T(8,128)(2,1)S(1)} %scatter.36, bf16[16,12,18,1]{3,0,2,1:T(8,128)(2,1)S(1)} %copy.735, s32[]{:T(128)} %constant.235.clone.1, s32[]{:T(128)} %constant.235.clone.1, s32[]{:T(128)} %constant.235.clone.1, s32[]{:T(128)} %constant.249.clone.1) | dynamic-update-slice | bytes 13828 | tf_op jit(solution)/shard_map/scatter | solution.py:97
  864.1 1.4 reshape.433
  865.5 162.9 %all-gather.5.cloned.1.call-done = bf16[128,12,18,34]{3,0,2,1:T(8,128)(2,1)} async-done(((bf16[16,12,18,34]{3,0,2,1:T(8,128)(2,1)}), bf16[128,12,18,34]{3,0,2,1:T(8,128)(2,1)}) %all-gather.5.cloned.1.call-update) | async-done | bytes 1880080 | tf_op jit(solution)/shard_map/all_gather | solution.py:158
  1028.4 4.8 fusion.2
  1034.3 1.9 fusion.10
  1037.2 1.9 fusion.14
  1039.1 1.9 fusion.4
  1040.9 1.9 fusion.8
  1042.8 1.3 fusion
  1044.1 2.3 add_convert_fusion
  1046.6 1.4 reshape.440
  (169 shorter events, 33.6 us)
Async XLA Ops:
  7.2 503.6 %copy-start = (bf16[3,3,128,128]{3,2,1,0:T(8,128)(2,1)S(1)}, bf16[3,3,128,128]{3,2,1,0:T(8,128)(2,1)}, u32[]{:S(2)}) copy-start(bf16[3,3,128,128]{3,2,1,0:T(8,128)(2,1)} %param.27) | copy-start | bytes 884740
  7.2 300.8 %all-reduce.3.cloned.1.call-start = ((), (), s32[]{:S(2)}) async-start(), calls=%async_computation | async-start | bytes 4194304 | tf_op jit(solution)/shard_map/psum | solution.py:75
  25.7 10.9 %copy-start.17 = (s32[12,4,3]{0,1,2:T(4,128)S(1)}, s32[12,4,3]{0,1,2:T(4,128)}, u32[]{:S(2)}) copy-start(s32[12,4,3]{0,1,2:T(4,128)} %param.28) | copy-start | bytes 1732
  25.7 12.0 %copy-start.26 = (s32[12,4,2]{0,2,1:T(2,128)S(1)}, s32[12,4,2]{0,2,1:T(2,128)}, u32[]{:S(2)}) copy-start(s32[12,4,2]{0,2,1:T(2,128)} %param.29) | copy-start | bytes 1156
  25.7 485.0 %all-gather.3.cloned.1.call-start = ((), (), s32[]{:S(2)}) async-start(), calls=%async_computation.1 | async-start | bytes 7962624 | tf_op jit(solution)/shard_map/all_gather | solution.py:151
  27.0 12.3 %collective-permute-start = (bf16[16,12,16,1]{2,0,3,1:T(8,128)(2,1)S(1)}, bf16[16,12,16,1]{2,0,3,1:T(8,128)(2,1)S(1)}, u32[]{:S(2)}, u32[]{:S(2)}) collective-permute-start(bf16[16,12,16,1]{2,0,3,1:T(8,128)(2,1)S(1)} %copy.684), channel_id=1, source_target_pairs={{0,64},{64,128},{128,192},{1,65},{65,129},{129,193},{2,66},{66,130... | collective-permute-start | bytes 18440 | tf_op jit(solution)/shard_map/ppermute | solution.py:16
  35.3 6.0 collective-permute-start.1
  43.6 5.9 collective-permute-start.2
  45.5 5.4 collective-permute-start.3
  49.5 1.4 copy-start.10
  50.9 0.6 copy-start.12
  53.1 258.7 %copy-start.15 = (pred[12]{0:T(512)(128)(4,1)S(1)}, pred[12]{0:T(512)(128)(4,1)}, u32[]{:S(2)}) copy-start(pred[12]{0:T(512)(128)(4,1)} %get-tuple-element.166) | copy-start | bytes 40
  53.1 259.6 %copy-start.13 = (pred[12]{0:T(512)(128)(4,1)S(1)}, pred[12]{0:T(512)(128)(4,1)}, u32[]{:S(2)}) copy-start(pred[12]{0:T(512)(128)(4,1)} %get-tuple-element.164) | copy-start | bytes 40
  311.0 4.6 copy-start.20
  311.0 4.7 copy-start.11
  311.0 4.9 copy-start.22
  313.8 3.6 copy-start.24
  322.7 2.5 copy-start.18
  345.1 1.0 copy-start.4
  346.1 479.3 %all-reduce.5.cloned.1.call-start = ((), (), s32[]{:S(2)}) async-start(), calls=%async_computation.2 | async-start | bytes 4194304 | tf_op jit(solution)/shard_map/psum | solution.py:75
  510.7 4.8 copy-start.2
  535.1 9.9 copy-start.7
  535.1 10.2 copy-start.6
  536.3 12.1 %collective-permute-start.4 = (bf16[16,12,16,1]{2,0,3,1:T(8,128)(2,1)S(1)}, bf16[16,12,16,1]{2,0,3,1:T(8,128)(2,1)S(1)}, u32[]{:S(2)}, u32[]{:S(2)}) collective-permute-start(bf16[16,12,16,1]{2,0,3,1:T(8,128)(2,1)S(1)} %copy.720), channel_id=1, source_target_pairs={{0,64},{64,128},{128,192},{1,65},{65,129},{129,193},{2,66},{66,130... | collective-permute-start | bytes 18440 | tf_op jit(solution)/shard_map/ppermute | solution.py:16
  539.8 9.9 collective-permute-start.5
  548.4 480.1 %all-gather.5.cloned.1.call-start = ((), (), s32[]{:S(2)}) async-start(), calls=%async_computation.3 | async-start | bytes 7962624 | tf_op jit(solution)/shard_map/all_gather | solution.py:158
  551.1 5.8 collective-permute-start.6
  553.0 5.4 collective-permute-start.7
  556.9 1.5 copy-start.8
  559.1 272.2 %copy-start.16 = (pred[12]{0:T(512)(128)(4,1)S(1)}, pred[12]{0:T(512)(128)(4,1)}, u32[]{:S(2)}) copy-start(pred[12]{0:T(512)(128)(4,1)} %get-tuple-element.166) | copy-start | bytes 40
  559.2 272.4 %copy-start.25 = (pred[12]{0:T(512)(128)(4,1)S(1)}, pred[12]{0:T(512)(128)(4,1)}, u32[]{:S(2)}) copy-start(pred[12]{0:T(512)(128)(4,1)} %get-tuple-element.162) | copy-start | bytes 40
  559.2 272.5 %copy-start.14 = (pred[12]{0:T(512)(128)(4,1)S(1)}, pred[12]{0:T(512)(128)(4,1)}, u32[]{:S(2)}) copy-start(pred[12]{0:T(512)(128)(4,1)} %get-tuple-element.164) | copy-start | bytes 40
  559.2 272.7 %copy-start.23 = (pred[12]{0:T(512)(128)(4,1)S(1)}, pred[12]{0:T(512)(128)(4,1)}, u32[]{:S(2)}) copy-start(pred[12]{0:T(512)(128)(4,1)} %get-tuple-element.161) | copy-start | bytes 40
  828.4 5.5 copy-start.21
  828.5 5.6 copy-start.9
  840.9 1.8 copy-start.19
  842.9 20.9 %copy-start.5 = (bf16[16,12,16,32]{3,0,2,1:T(8,128)(2,1)S(1)}, bf16[16,12,16,32]{3,0,2,1:T(8,128)(2,1)}, u32[]{:S(2)}) copy-start(bf16[16,12,16,32]{3,0,2,1:T(8,128)(2,1)} %get-tuple-element.139) | copy-start | bytes 589828
  862.8 1.0 copy-start.3
  1028.4 4.8 copy-start.1
Sparse Core Ops, SparseCore 0:
  25.8 282.0 all-reduce.2
  346.2 164.4 all-gather.2
  548.5 276.8 all-reduce.4
  863.9 164.4 all-gather.4
where the time goes:
time: 1060 us
  waiting for transfers between devices  850 us (80%)
  local copies, waits for them, and re-layouts  117 us (11%)
  matrix products  36.3 us (3%)
  starting transfers between devices  24 us (2%)
  between operations  15.2 us (1%)
  other arithmetic  12.9 us (1%)
    psum x2, waiting for transfers between devices, face_lines_of(): return lax.psum(contrib.astype(jnp.bfloat16), ('px', 'py'))  521 us
    all_gather x1, waiting for transfers between devices, local(): lax.all_gather(grad_pad, 'ch', axis=0, tiled=True)  163 us
    all_gather x1, waiting for transfers between devices, local(): lax.all_gather(feat_pad, 'ch', axis=0, tiled=True)  163 us
    scatter x2, local copies, waits for them, and re-layouts, pad_field(): padded.at[:, :, :, -1]  36.9 us
  transfers between devices with their start and end apart: 12, of which 7 were waited for; matrix products, arithmetic and copies ran while one was open for 2% of the time, Pallas kernels for 0%

commit v1 on v0

--- a/solution.py
+++ b/solution.py
@@ -4,6 +4,11 @@
 from jax.sharding import PartitionSpec as P
 
 RB = 32
+
+
+def swapped_in(x, axis, along):
+    outgoing = jnp.stack([x] * lax.axis_size(axis))
+    return jnp.concatenate(lax.all_to_all(outgoing, axis, 0, 0), axis=along)
 
 
 def with_halo(array, sides, width):
@@ -154,9 +159,9 @@
     grad_pad = pad_field(gated, edge_table, corner_table)
     input_taps = lax.dynamic_slice_in_dim(weight, ch_pos * chan_block, chan_block, 3)
     piece_taps = input_taps
-    input_grad = backward_taps(
-        lax.all_gather(grad_pad, "ch", axis=0, tiled=True), piece_taps, col_len, row_len
-    ).astype(jnp.bfloat16)
+    input_grad = backward_taps(swapped_in(grad_pad, "ch", 0), piece_taps, col_len, row_len).astype(
+        jnp.bfloat16
+    )
     out_shape = (chan_block, face_count, 1, 1, tile_len)
     return (activation.reshape(out_shape), input_grad.reshape(out_shape))
 

time: 1060 us -> 985 us (0.929); the launches traced: 1060 us -> 967 us
  waiting for transfers between devices: 850 us -> 709 us
  local copies, waits for them, and re-layouts: 117 us -> 164 us
    all_gather x1 -> x0, waiting for transfers between devices: 163 us -> none  [local(): lax.all_gather(grad_pad, 'ch', axis=0, tiled=True)]
    unnamed x54 -> x51, local copies, waits for them, and re-layouts: 2.85 us -> 43.9 us
    all_to_all x0 -> x1, waiting for transfers between devices: none -> 21.7 us  [swapped_in(): return jnp.concatenate(lax.all_to_all(outgoing, axis, 0, 0), axis=along)]
    scatter x2 -> x3, local copies, waits for them, and re-layouts: 36.9 us -> 37.9 us  [pad_field(): padded.at[:, :, :, -1]]
  transfers between devices with their start and end apart: 12 -> 12, of which waited for: 7 -> 7; matrix products, arithmetic and copies ran while one was open for 2% -> 3% of each run, Pallas kernels for 0% -> 0%
where the time goes in v1:
time: 985 us; the launch traced here: 967 us
  waiting for transfers between devices  709 us (72%)
  local copies, waits for them, and re-layouts  164 us (17%)
  matrix products  33.7 us (3%)
  starting transfers between devices  33.1 us (3%)
  between operations  15.2 us (2%)
  other arithmetic  12.8 us (1%)
    psum x2, waiting for transfers between devices, face_lines_of(): return lax.psum(contrib.astype(jnp.bfloat16), ('px', 'py'))  521 us
    all_gather x1, waiting for transfers between devices, local(): lax.all_gather(feat_pad, 'ch', axis=0, tiled=True)  163 us
    unnamed x51, local copies, waits for them, and re-layouts  43.9 us
    scatter x3, local copies, waits for them, and re-layouts, pad_field(): padded.at[:, :, :, -1]  37.9 us
    all_to_all x1, waiting for transfers between devices, swapped_in(): return jnp.concatenate(lax.all_to_all(outgoing, axis, 0, 0), axis=along)  21.7 us
  transfers between devices with their start and end apart: 12, of which 7 were waited for; matrix products, arithmetic and copies ran while one was open for 3% of the time, Pallas kernels for 0%

profile of v1, /device:TPU:8, one launch (start us, length us, event | category | flops | bytes accessed | tf_op | source)
XLA Modules:
  0.0 967.1 jit_solution(11605734247841137968)
XLA Ops:
  7.2 1.4 reshape.434
  9.9 1.4 convert_select_fusion.2
  11.2 3.0 copy.696
  14.2 1.8 copy.697
  16.0 2.7 select_n.196
  18.7 2.7 select_n.200
  23.0 2.6 copy.698
  26.9 7.1 collective-permute-start
  35.2 1.3 collective-permute-start.1
  39.3 1.6 copy.687
  41.2 1.6 copy.689
  43.5 1.9 collective-permute-start.2
  45.5 4.2 collective-permute-start.3
  51.5 1.6 pad_maximum_fusion
  53.1 254.8 %all-reduce.3.cloned.1.call-done = bf16[16,12,4,128]{1,0,3,2:T(8,128)(2,1)} async-done(((bf16[16,12,4,128]{1,0,3,2:T(8,128)(2,1)}), bf16[16,12,4,128]{1,0,3,2:T(8,128)(2,1)}) %all-reduce.3.cloned.1.call-update) | async-done | bytes 196624 | tf_op jit(solution)/shard_map/psum | solution.py:80
  307.9 3.0 copy.702
  317.6 1.3 copy.705
  318.9 3.8 scatter.34
  325.4 1.3 copy.707
  326.7 18.3 %scatter.35 = bf16[16,12,18,34]{3,0,2,1:T(8,128)(2,1)S(1)} dynamic-update-slice(bf16[16,12,18,34]{3,0,2,1:T(8,128)(2,1)S(1)} %scatter.34, bf16[16,12,18,1]{3,0,2,1:T(8,128)(2,1)S(1)} %copy.707, s32[]{:T(128)} %constant.237.clone.1, s32[]{:T(128)} %constant.237.clone.1, s32[]{:T(128)} %constant.237.clone.1, s32[]{:T(128)} %constant.251.clone.1) | dynamic-update-slice | bytes 13828 | tf_op jit(solution)/shard_map/scatter | solution.py:102
  346.3 1.3 reshape.449
  347.7 163.0 %all-gather.2.cloned.1.call-done = bf16[128,12,18,34]{3,0,2,1:T(8,128)(2,1)} async-done(((bf16[16,12,18,34]{3,0,2,1:T(8,128)(2,1)}), bf16[128,12,18,34]{3,0,2,1:T(8,128)(2,1)}) %all-gather.2.cloned.1.call-update) | async-done | bytes 1880080 | tf_op jit(solution)/shard_map/all_gather | solution.py:156
  510.7 4.7 fusion.20
  515.5 1.8 fusion.24
  518.2 1.8 fusion.26
  521.0 1.8 fusion.30
  522.8 1.8 fusion.32
  524.6 2.2 fusion.18
  526.8 2.5 fusion.37
  529.4 1.7 convert_select_fusion.1
  531.7 2.3 copy.725
  536.5 2.2 collective-permute-start.4
  539.9 1.3 collective-permute-start.5
  541.2 1.9 select_n.220
  543.2 1.9 select_n.223
  545.8 2.6 copy.727
  548.5 1.3 copy.722
  549.8 1.3 copy.723
  551.2 1.9 collective-permute-start.6
  553.1 3.8 collective-permute-start.7
  557.0 1.5 collective-permute-done.7
  559.3 266.3 %all-reduce.5.cloned.1.call-done = bf16[16,12,4,128]{1,0,3,2:T(8,128)(2,1)} async-done(((bf16[16,12,4,128]{1,0,3,2:T(8,128)(2,1)}), bf16[16,12,4,128]{1,0,3,2:T(8,128)(2,1)}) %all-reduce.5.cloned.1.call-update) | async-done | bytes 196624 | tf_op jit(solution)/shard_map/psum | solution.py:80
  825.5 3.0 copy.731
  834.5 1.3 copy.732
  835.9 1.3 copy.733
  837.2 3.8 scatter.48
  843.0 1.3 copy.735
  844.3 18.3 %scatter.50 = bf16[16,12,18,34]{3,0,2,1:T(8,128)(2,1)S(1)} dynamic-update-slice(bf16[16,12,18,34]{3,0,2,1:T(8,128)(2,1)S(1)} %scatter.48, bf16[16,12,18,1]{3,0,2,1:T(8,128)(2,1)S(1)} %copy.735, s32[]{:T(128)} %constant.237.clone.1, s32[]{:T(128)} %constant.237.clone.1, s32[]{:T(128)} %constant.237.clone.1, s32[]{:T(128)} %constant.251.clone.1) | dynamic-update-slice | bytes 13828 | tf_op jit(solution)/shard_map/scatter | solution.py:102
  862.6 4.0 broadcast_bitcast_fusion
  866.7 15.8 %reshape.584 = bf16[8,2,58752]{2,1,0:T(2,128)(2,1)} reshape(bf16[8,12,18,16,34]{4,3,2,1,0:T(8,128)(2,1)} %broadcast_bitcast_fusion) | data formatting | bytes 3760128
  882.5 9.1 all-to-all-start
  891.6 1.3 copy.717
  892.9 1.5 reshape.441
  894.4 21.7 %all-to-all-done = bf16[8,2,58752]{2,1,0:T(2,128)(2,1)S(1)} async-done(((bf16[8,2,58752]{2,1,0:T(2,128)(2,1)}), bf16[8,2,58752]{2,1,0:T(2,128)(2,1)S(1)}, u32[]{:S(2)}, u32[]{:S(2)}) %all-to-all-start) | async-done | bytes 1880096 | tf_op jit(solution)/shard_map/all_to_all | solution.py:11
  916.1 22.2 %reshape.585 = bf16[8,12,18,16,34]{4,3,2,1,0:T(8,128)(2,1)} reshape(bf16[8,2,58752]{2,1,0:T(2,128)(2,1)S(1)} %all-to-all-done) | data formatting | bytes 3760128
  938.3 5.1 copy.736
  943.4 1.9 fusion.2
  946.3 1.9 fusion.10
  949.3 1.9 fusion.14
  951.1 1.9 fusion.4
  953.0 1.9 fusion.8
  954.8 1.3 fusion
  956.1 2.4 add_convert_fusion
  958.7 1.4 reshape.448
  (166 shorter events, 39.3 us)
Async XLA Ops:
  7.2 503.5 %copy-start = (bf16[3,3,128,128]{3,2,1,0:T(8,128)(2,1)S(1)}, bf16[3,3,128,128]{3,2,1,0:T(8,128)(2,1)}, u32[]{:S(2)}) copy-start(bf16[3,3,128,128]{3,2,1,0:T(8,128)(2,1)} %param.27) | copy-start | bytes 884740
  7.2 300.7 %all-reduce.3.cloned.1.call-start = ((), (), s32[]{:S(2)}) async-start(), calls=%async_computation.1 | async-start | bytes 4194304 | tf_op jit(solution)/shard_map/psum | solution.py:80
  25.7 10.9 %copy-start.14 = (s32[12,4,3]{0,1,2:T(4,128)S(1)}, s32[12,4,3]{0,1,2:T(4,128)}, u32[]{:S(2)}) copy-start(s32[12,4,3]{0,1,2:T(4,128)} %param.28) | copy-start | bytes 1732
  25.7 12.0 %copy-start.23 = (s32[12,4,2]{0,2,1:T(2,128)S(1)}, s32[12,4,2]{0,2,1:T(2,128)}, u32[]{:S(2)}) copy-start(s32[12,4,2]{0,2,1:T(2,128)} %param.29) | copy-start | bytes 1156
  25.7 485.0 %all-gather.2.cloned.1.call-start = ((), (), s32[]{:S(2)}) async-start(), calls=%async_computation.2 | async-start | bytes 7962624 | tf_op jit(solution)/shard_map/all_gather | solution.py:156
  26.9 12.4 %collective-permute-start = (bf16[16,12,16,1]{2,0,3,1:T(8,128)(2,1)S(1)}, bf16[16,12,16,1]{2,0,3,1:T(8,128)(2,1)S(1)}, u32[]{:S(2)}, u32[]{:S(2)}) collective-permute-start(bf16[16,12,16,1]{2,0,3,1:T(8,128)(2,1)S(1)} %copy.684), channel_id=1, source_target_pairs={{0,64},{64,128},{128,192},{1,65},{65,129},{129,193},{2,66},{66,130... | collective-permute-start | bytes 18440 | tf_op jit(solution)/shard_map/ppermute | solution.py:21
  35.2 6.0 collective-permute-start.1
  43.5 6.2 collective-permute-start.2
  45.5 5.4 collective-permute-start.3
  49.8 1.1 copy-start.7
  50.9 0.6 copy-start.9
  53.1 258.7 %copy-start.12 = (pred[12]{0:T(512)(128)(4,1)S(1)}, pred[12]{0:T(512)(128)(4,1)}, u32[]{:S(2)}) copy-start(pred[12]{0:T(512)(128)(4,1)} %get-tuple-element.166) | copy-start | bytes 40
  53.1 259.6 %copy-start.10 = (pred[12]{0:T(512)(128)(4,1)S(1)}, pred[12]{0:T(512)(128)(4,1)}, u32[]{:S(2)}) copy-start(pred[12]{0:T(512)(128)(4,1)} %get-tuple-element.164) | copy-start | bytes 40
  53.1 262.4 %copy-start.17 = (pred[12]{0:T(512)(128)(4,1)S(1)}, pred[12]{0:T(512)(128)(4,1)}, u32[]{:S(2)}) copy-start(pred[12]{0:T(512)(128)(4,1)} %get-tuple-element.163) | copy-start | bytes 40
  311.0 4.7 copy-start.8
  311.0 4.8 copy-start.19
  312.8 4.5 copy-start.21
  322.7 2.5 copy-start.15
  345.0 1.0 copy-start.2
  346.1 479.5 %all-reduce.5.cloned.1.call-start = ((), (), s32[]{:S(2)}) async-start(), calls=%async_computation.3 | async-start | bytes 4194304 | tf_op jit(solution)/shard_map/psum | solution.py:80
  510.7 4.8 copy-start.1
  535.3 9.9 %copy-start.4 = (bf16[16,12,1,32]{3,0,2,1:T(8,128)(2,1)S(1)}, bf16[16,12,1,32]{3,0,2,1:T(8,128)(2,1)}, u32[]{:S(2)}) copy-start(bf16[16,12,1,32]{3,0,2,1:T(8,128)(2,1)} %get-tuple-element.140) | copy-start | bytes 36868
  535.3 10.2 %copy-start.3 = (bf16[16,12,1,32]{3,0,2,1:T(8,128)(2,1)S(1)}, bf16[16,12,1,32]{3,0,2,1:T(8,128)(2,1)}, u32[]{:S(2)}) copy-start(bf16[16,12,1,32]{3,0,2,1:T(8,128)(2,1)} %get-tuple-element.141) | copy-start | bytes 36868
  536.5 12.0 %collective-permute-start.4 = (bf16[16,12,16,1]{2,0,3,1:T(8,128)(2,1)S(1)}, bf16[16,12,16,1]{2,0,3,1:T(8,128)(2,1)S(1)}, u32[]{:S(2)}, u32[]{:S(2)}) collective-permute-start(bf16[16,12,16,1]{2,0,3,1:T(8,128)(2,1)S(1)} %copy.720), channel_id=1, source_target_pairs={{0,64},{64,128},{128,192},{1,65},{65,129},{129,193},{2,66},{66,130... | collective-permute-start | bytes 18440 | tf_op jit(solution)/shard_map/ppermute | solution.py:21
  539.9 9.9 %collective-permute-start.5 = (bf16[16,12,16,1]{2,0,3,1:T(8,128)(2,1)S(1)}, bf16[16,12,16,1]{2,0,3,1:T(8,128)(2,1)S(1)}, u32[]{:S(2)}, u32[]{:S(2)}) collective-permute-start(bf16[16,12,16,1]{2,0,3,1:T(8,128)(2,1)S(1)} %copy.721), channel_id=1, source_target_pairs={{64,0},{128,64},{192,128},{65,1},{129,65},{193,129},{66,2},{130,66... | collective-permute-start | bytes 18440 | tf_op jit(solution)/shard_map/ppermute | solution.py:22
  551.2 5.8 collective-permute-start.6
  553.1 5.4 collective-permute-start.7
  556.9 1.5 copy-start.5
  559.2 272.3 %copy-start.13 = (pred[12]{0:T(512)(128)(4,1)S(1)}, pred[12]{0:T(512)(128)(4,1)}, u32[]{:S(2)}) copy-start(pred[12]{0:T(512)(128)(4,1)} %get-tuple-element.166) | copy-start | bytes 40
  559.2 272.5 %copy-start.22 = (pred[12]{0:T(512)(128)(4,1)S(1)}, pred[12]{0:T(512)(128)(4,1)}, u32[]{:S(2)}) copy-start(pred[12]{0:T(512)(128)(4,1)} %get-tuple-element.162) | copy-start | bytes 40
  559.3 272.6 %copy-start.11 = (pred[12]{0:T(512)(128)(4,1)S(1)}, pred[12]{0:T(512)(128)(4,1)}, u32[]{:S(2)}) copy-start(pred[12]{0:T(512)(128)(4,1)} %get-tuple-element.164) | copy-start | bytes 40
  559.3 272.7 %copy-start.20 = (pred[12]{0:T(512)(128)(4,1)S(1)}, pred[12]{0:T(512)(128)(4,1)}, u32[]{:S(2)}) copy-start(pred[12]{0:T(512)(128)(4,1)} %get-tuple-element.161) | copy-start | bytes 40
  828.6 5.5 copy-start.18
  828.6 5.6 copy-start.6
  841.0 1.8 copy-start.16
  882.5 33.6 %all-to-all-start = ((bf16[8,2,58752]{2,1,0:T(2,128)(2,1)}), bf16[8,2,58752]{2,1,0:T(2,128)(2,1)S(1)}, u32[]{:S(2)}, u32[]{:S(2)}) async-start(bf16[8,2,58752]{2,1,0:T(2,128)(2,1)} %reshape.584), calls=%async_computation | async-start | bytes 3760128 | tf_op jit(solution)/shard_map/all_to_all | solution.py:11
Sparse Core Ops, SparseCore 0:
  25.8 282.0 all-reduce.2
  346.2 164.4 all-gather.1
  548.6 276.8 all-reduce.4
